TPU v7x, 32 devices: a whole 2x2x4 slice. The times are simulated.
32 devices in a mesh: layer: 2 (over y), feat: 4 (over x, core), width: 4 (over z).
Axes of the slice: x: 2, y: 2, z: 4, core: 2. Of those that a mesh axis runs over, the one named last changes fastest.
Arguments:
- resid: bfloat16 [2, 128, 2048], P(None, 'layer', 'width'), may hold values from -6 to 6
- enc_w: bfloat16 [2, 2048, 65536], P(None, 'width', ('layer', 'feat')), may hold values from -0.125 to 0.125
- enc_b: float32 [2, 65536], P(None, ('layer', 'feat')), may hold values from -3 to 3
- dec_w: float32 [3, 65536, 2048], P(None, ('layer', 'feat'), 'width'), may hold values from -0.03125 to 0.03125
- dec_b: float32 [2, 2048], P(None, 'width'), may hold values from -2 to 2
- target: float32 [2, 128, 2048], P(None, ('layer', 'feat'), 'width'), may hold values from -6 to 6
Outputs:
- recon: float32 [2, 128, 2048], P(None, ('layer', 'feat'), 'width')
- err: float32 [2, 128], P(None, ('layer', 'feat'))
All inputs are finite; a program needn't handle non-finite values.
Results may differ from a plain program's by a relative error of at most 0.00035.
Values may be sent and summed in bfloat16 or wider, within the bound.
No kernel may reach another device: no remote copies, remote signals or barrier semaphores. Data moves between devices by JAX's collectives and lax.ppermute only.
A program may use at most 128 MiB of HBM per device.

v0:
```python
import jax
import jax.numpy as jnp
from jax import lax
from jax.sharding import PartitionSpec as P


def decode_rows(act, dec_w, target_idx):
    total = None
    for layer_idx in range(target_idx + 1):
        block = target_idx * (target_idx + 1) // 2 + layer_idx
        rows = act[layer_idx]
        term = jnp.dot(
            rows, dec_w[block], precision=lax.Precision.HIGHEST, preferred_element_type=jnp.float32
        )
        total = term if total is None else total + term
    return total


def per_device(resid, enc_w, enc_b, dec_w, dec_b, target):
    layers = resid.shape[0]
    gathered = lax.all_gather(resid, "layer", axis=1, tiled=True)
    tokens = gathered.shape[1]
    partial_pre = jnp.einsum("ltd,ldf->ltf", gathered, enc_w, preferred_element_type=jnp.float32)
    pre = lax.psum(partial_pre, "width")
    act = jnp.maximum(pre + enc_b[:, None, :], 0.0)
    own_rows = tokens // lax.axis_size(("layer", "feat"))
    summed = lax.psum_scatter(
        jnp.concatenate(
            [decode_rows(act, dec_w, target_idx) for target_idx in range(layers)], axis=1
        ),
        ("layer", "feat"),
        scatter_dimension=0,
        tiled=True,
    )
    summed = summed.reshape(own_rows, layers, dec_w.shape[2]).transpose(1, 0, 2)
    recon = summed + dec_b[:, None, :]
    diff = recon - target
    sq_error, sq_target = lax.psum(
        (jnp.sum(diff * diff, axis=2), jnp.sum(target * target, axis=2)), "width"
    )
    err = sq_error / (sq_target + 1e-06)
    return (recon, err)


def solution(mesh):
    in_specs = (
        P(None, "layer", "width"),
        P(None, "width", ("layer", "feat")),
        P(None, ("layer", "feat")),
        P(None, ("layer", "feat"), "width"),
        P(None, "width"),
        P(None, ("layer", "feat"), "width"),
    )
    out_specs = (P(None, ("layer", "feat"), "width"), P(None, ("layer", "feat")))
    return jax.shard_map(
        per_device, mesh=mesh, in_specs=in_specs, out_specs=out_specs, check_vma=False
    )
```

profile of v0, /device:TPU:0, one launch (start us, length us, event | category | flops | bytes accessed | tf_op | source)
XLA Modules:
  0.0 413.2 jit_solution(15221711624656479680)
XLA Ops:
  7.2 0.0 all-reduce.3.cloned.1.call-start
  7.2 7.4 %all_gather.3 = bf16[2,128,512]{2,1,0:T(8,128)(2,1)S(1)} all-gather(bf16[2,64,512]{2,1,0:T(8,128)(2,1)} %param.6), channel_id=1, replica_groups=mesh['layer'=2,'feat'=4,'width'=4] {'layer'}, dimensions={1}, use_global_device_ids=true | all-gather | bytes 393216 | tf_op jit(solution)/shard_map/all_gather | solution.py:21
  14.6 11.3 %fusion.14 = f32[2,128,8192]{2,1,0:T(8,128)} fusion(bf16[2,128,512]{2,1,0:T(8,128)(2,1)S(1)} %all_gather.3, bf16[2,512,8192]{2,1,0:T(8,128)(2,1)} %param.7), kind=kOutput, calls=%fused_computation.19 | convolution fusion | flops 2147483648 | bytes 25427968 | tf_op jit(solution)/shard_map/ltd,ldf->ltf/dot_general | solution.py:23
  26.0 0.0 copy-start
  26.0 0.0 all-reduce.3.cloned.1.call-update
  26.0 0.0 reduce-scatter.2.cloned.1.call-start
  26.0 292.4 %all-reduce.3.cloned.1.call-done = f32[2,128,8192]{2,1,0:T(8,128)} async-done(((f32[2,128,8192]{2,1,0:T(8,128)}), f32[2,128,8192]{2,1,0:T(8,128)}) %all-reduce.3.cloned.1.call-update) | async-done | bytes 8388624 | tf_op jit(solution)/shard_map/psum | solution.py:24
  318.4 0.0 copy-done
  318.4 4.2 %add_maximum_fusion = f32[2,128,8192]{2,1,0:T(8,128)S(1)} fusion(f32[2,128,8192]{2,1,0:T(8,128)} %all-reduce.3.cloned.1.call-done, f32[2,8192]{1,0:T(2,128)S(1)} %copy-done), kind=kLoop, calls=%fused_computation.9 | loop fusion | flops 4194304 | bytes 16842752 | tf_op jit(solution)/shard_map/max | solution.py:25
  322.6 11.9 %fusion = f32[128,512]{1,0:T(8,128)S(1)} fusion(f32[3,8192,512]{2,1,0:T(8,128)} %param.9, f32[2,128,8192]{2,1,0:T(8,128)S(1)} %add_maximum_fusion), kind=kOutput, calls=%fused_computation | convolution fusion | flops 6442450944 | bytes 21233664 | tf_op jit(solution)/shard_map/dot_general | solution.py:12
  334.5 11.9 %fusion.4 = f32[128,512]{1,0:T(8,128)S(1)} fusion(f32[3,8192,512]{2,1,0:T(8,128)} %param.9, f32[2,128,8192]{2,1,0:T(8,128)S(1)} %add_maximum_fusion), kind=kOutput, calls=%fused_computation.4 | convolution fusion | flops 6442450944 | bytes 21233664 | tf_op jit(solution)/shard_map/dot_general | solution.py:12
  346.4 0.0 copy-start.1
  346.4 0.0 copy-start.2
  346.4 12.1 %fusion.9 = f32[128,512]{1,0:T(8,128)S(1)} fusion(f32[128,512]{1,0:T(8,128)S(1)} %fusion, f32[3,8192,512]{2,1,0:T(8,128)} %param.9, f32[2,128,8192]{2,1,0:T(8,128)S(1)} %add_maximum_fusion), kind=kOutput, calls=%fused_computation.12 | convolution fusion | flops 6442516480 | bytes 21495808 | tf_op jit(solution)/shard_map/dot_general | solution.py:12
  358.5 0.8 pad_maximum_fusion
  359.3 0.0 reduce-scatter.2.cloned.1.call-update
  359.4 33.2 %reduce-scatter.2.cloned.1.call-done = f32[16,1024]{1,0:T(8,128)} async-done(((f32[128,1024]{1,0:T(8,128)}), f32[16,1024]{1,0:T(8,128)}) %reduce-scatter.2.cloned.1.call-update) | async-done | bytes 65552 | tf_op jit(solution)/shard_map/reduce_scatter | solution.py:27
  392.6 0.0 copy-done.1
  392.6 0.0 copy-done.2
  392.6 1.5 multiply_reduce_fusion
  394.1 11.6 %all-reduce = (f32[2,16]{1,0:T(2,128)S(1)}, f32[2,16]{1,0:T(2,128)S(1)}) all-reduce(f32[2,16]{1,0:T(2,128)S(1)} %get-tuple-element.3, f32[2,16]{1,0:T(2,128)S(1)} %get-tuple-element.2), channel_id=1, replica_groups=mesh['layer'=2,'feat'=4,'width'=4] {'width'}, use_global_device_ids=true, to_apply=%region_3.0 | all-reduce | flops 64 | bytes 512 | tf_op jit(solution)/shard_map/psum | solution.py:38
  405.8 0.6 add_divide_fusion
Async XLA Ops:
  7.2 311.2 %all-reduce.3.cloned.1.call-start = ((), (), s32[]{:S(2)}) async-start(), calls=%async_computation.1 | async-start | bytes 16777216 | tf_op jit(solution)/shard_map/psum | solution.py:24
  26.0 292.4 %copy-start = (f32[2,8192]{1,0:T(2,128)S(1)}, f32[2,8192]{1,0:T(2,128)}, u32[]{:S(2)}) copy-start(f32[2,8192]{1,0:T(2,128)} %param.8) | copy-start | bytes 196612
  26.0 366.6 %reduce-scatter.2.cloned.1.call-start = ((), (), s32[]{:S(2)}) async-start(), calls=%async_computation.2 | async-start | bytes 589824 | tf_op jit(solution)/shard_map/reduce_scatter | solution.py:27
  346.4 46.2 %copy-start.1 = (f32[2,16,512]{2,1,0:T(8,128)S(1)}, f32[2,16,512]{2,1,0:T(8,128)}, u32[]{:S(2)}) copy-start(f32[2,16,512]{2,1,0:T(8,128)} %param.11) | copy-start | bytes 196612
  346.4 46.2 %copy-start.2 = (f32[2,512]{1,0:T(2,128)S(1)}, f32[2,512]{1,0:T(2,128)}, u32[]{:S(2)}) copy-start(f32[2,512]{1,0:T(2,128)} %param.10) | copy-start | bytes 12292
Sparse Core Ops, SparseCore 0:
  26.1 292.2 all-reduce.2
  359.5 33.0 reduce-scatter.1
where the time goes:
time: 413 us
  waiting for transfers between devices  326 us (79%)
  matrix products  47.2 us (11%)
  blocking collectives  19.1 us (5%)
  between operations  14.1 us (3%)
  other arithmetic  7.07 us (2%)
    psum x1, waiting for transfers between devices, per_device(): pre = lax.psum(partial_pre, 'width')  292 us
    dot_general x3, matrix products, decode_rows(): jnp.dot(rows, dec_w[block], precision=lax.Precision.HIGHEST, preferred_el...  35.9 us
    reduce_scatter x1, waiting for transfers between devices, per_device(): lax.psum_scatter(jnp.concatenate([decode_rows(act, dec_w, target_idx) for...  33.2 us
    psum x1, blocking collectives, per_device(): lax.psum((jnp.sum(diff * diff, axis=2), jnp.sum(target * target, axis=2))...  11.6 us
    dot_general x1, matrix products, per_device(): jnp.einsum('ltd,ldf->ltf', gathered, enc_w, preferred_element_type=jnp.fl...  11.3 us
  transfers between devices with their start and end apart: 2, of which 2 were waited for; matrix products, arithmetic and copies ran while one was open for 0% of the time, Pallas kernels for 0%

commit v1 on v0

--- a/solution.py
+++ b/solution.py
@@ -21,7 +21,9 @@
     gathered = lax.all_gather(resid, "layer", axis=1, tiled=True)
     tokens = gathered.shape[1]
     partial_pre = jnp.einsum("ltd,ldf->ltf", gathered, enc_w, preferred_element_type=jnp.float32)
-    pre = lax.psum(partial_pre, "width")
+    pre = partial_pre
+    for hop in (1, 2):
+        pre = pre + lax.ppermute(pre, "width", [(dev, dev ^ hop) for dev in range(4)])
     act = jnp.maximum(pre + enc_b[:, None, :], 0.0)
     own_rows = tokens // lax.axis_size(("layer", "feat"))
     summed = lax.psum_scatter(

time: 413 us -> 684 us (1.66)
  waiting for transfers between devices: 326 us -> 574 us
  other arithmetic: 7.07 us -> 24.2 us
    ppermute x0 -> x2, waiting for transfers between devices: none -> 539 us  [per_device(): lax.ppermute(pre, 'width', [(dev, dev ^ hop) for dev in range(4)])]
    psum x1 -> x0, waiting for transfers between devices: 292 us -> none  [per_device(): pre = lax.psum(partial_pre, 'width')]
    add x0 -> x1, other arithmetic: none -> 10.3 us  [per_device(): pre + lax.ppermute(pre, 'width', [(dev, dev ^ hop) for dev in range(4)])]
    max x1, other arithmetic: 4.19 us -> 11.1 us  [per_device(): act = jnp.maximum(pre + enc_b[:, None, :], 0.0)]
  transfers between devices with their start and end apart: 2 -> 3, of which waited for: 2 -> 3; matrix products, arithmetic and copies ran while one was open for 0% -> 0% of each run, Pallas kernels for 0% -> 0%
where the time goes in v1:
time: 684 us
  waiting for transfers between devices  574 us (84%)
  matrix products  45.1 us (7%)
  other arithmetic  24.2 us (4%)
  blocking collectives  19.1 us (3%)
  between operations  14.1 us (2%)
    ppermute x2, waiting for transfers between devices, per_device(): lax.ppermute(pre, 'width', [(dev, dev ^ hop) for dev in range(4)])  539 us
    dot_general x3, matrix products, decode_rows(): jnp.dot(rows, dec_w[block], precision=lax.Precision.HIGHEST, preferred_el...  36.9 us
    reduce_scatter x1, waiting for transfers between devices, per_device(): lax.psum_scatter(jnp.concatenate([decode_rows(act, dec_w, target_idx) for...  35 us
  transfers between devices with their start and end apart: 3, of which 3 were waited for; matrix products, arithmetic and copies ran while one was open for 0% of the time, Pallas kernels for 0%

profile of v1, /device:TPU:0, one launch (start us, length us, event | category | flops | bytes accessed | tf_op | source)
XLA Modules:
  0.0 684.2 jit_solution(14321457187715697947)
XLA Ops:
  7.2 0.0 reduce-scatter.2.cloned.1.call-start
  7.2 7.4 %all_gather.3 = bf16[2,128,512]{2,1,0:T(8,128)(2,1)S(1)} all-gather(bf16[2,64,512]{2,1,0:T(8,128)(2,1)} %param.6), channel_id=1, replica_groups=mesh['layer'=2,'feat'=4,'width'=4] {'layer'}, dimensions={1}, use_global_device_ids=true | all-gather | bytes 393216 | tf_op jit(solution)/shard_map/all_gather | solution.py:21
  14.6 8.1 %fusion.14 = f32[2,128,8192]{2,1,0:T(8,128)S(1)} fusion(bf16[2,128,512]{2,1,0:T(8,128)(2,1)S(1)} %all_gather.3, bf16[2,512,8192]{2,1,0:T(8,128)(2,1)} %param.7), kind=kOutput, calls=%fused_computation.19 | convolution fusion | flops 2147483648 | bytes 25427968 | tf_op jit(solution)/shard_map/ltd,ldf->ltf/dot_general | solution.py:23
  22.8 0.0 copy-start
  22.8 3.2 copy-done
  26.0 0.0 copy-start.2
  26.0 1.7 collective-permute-start
  27.7 180.0 %collective-permute-done = f32[2,128,8192]{2,1,0:T(8,128)} collective-permute-done((f32[2,128,8192]{2,1,0:T(8,128)S(1)}, f32[2,128,8192]{2,1,0:T(8,128)}, u32[]{:S(2)}, u32[]{:S(2)}) %collective-permute-start) | collective-permute-done | bytes 8388640 | tf_op jit(solution)/shard_map/ppermute | solution.py:26
  207.7 10.3 %add.40 = f32[2,128,8192]{2,1,0:T(8,128)} add(f32[2,128,8192]{2,1,0:T(8,128)} %copy-done, f32[2,128,8192]{2,1,0:T(8,128)} %collective-permute-done) | non-fusion elementwise | flops 2097152 | bytes 25165824 | tf_op jit(solution)/shard_map/add | solution.py:26
  218.0 2.5 collective-permute-start.1
  220.4 359.3 %collective-permute-done.1 = f32[2,128,8192]{2,1,0:T(8,128)} collective-permute-done((f32[2,128,8192]{2,1,0:T(8,128)}, f32[2,128,8192]{2,1,0:T(8,128)}, u32[]{:S(2)}, u32[]{:S(2)}) %collective-permute-start.1) | collective-permute-done | bytes 8388640 | tf_op jit(solution)/shard_map/ppermute | solution.py:26
  579.7 0.0 copy-done.2
  579.7 11.1 %add_maximum_fusion = f32[2,128,8192]{2,1,0:T(8,128)} fusion(f32[2,128,8192]{2,1,0:T(8,128)} %add.40, f32[2,128,8192]{2,1,0:T(8,128)} %collective-permute-done.1, f32[2,8192]{1,0:T(2,128)S(1)} %copy-done.2), kind=kLoop, calls=%fused_computation.9 | loop fusion | flops 6291456 | bytes 25231360 | tf_op jit(solution)/shard_map/max | solution.py:27
  590.8 0.0 copy-start.1
  590.8 12.9 %fusion = f32[128,512]{1,0:T(8,128)S(1)} fusion(f32[3,8192,512]{2,1,0:T(8,128)} %param.9, f32[2,128,8192]{2,1,0:T(8,128)} %add_maximum_fusion), kind=kOutput, calls=%fused_computation | convolution fusion | flops 6442450944 | bytes 21233664 | tf_op jit(solution)/shard_map/dot_general | solution.py:12
  603.7 0.0 copy-done.1
  603.8 11.9 %fusion.4 = f32[128,512]{1,0:T(8,128)S(1)} fusion(f32[3,8192,512]{2,1,0:T(8,128)} %param.9, f32[2,128,8192]{2,1,0:T(8,128)S(1)} %copy-done.1), kind=kOutput, calls=%fused_computation.4 | convolution fusion | flops 6442450944 | bytes 21233664 | tf_op jit(solution)/shard_map/dot_general | solution.py:12
  615.6 0.0 copy-start.3
  615.6 0.0 copy-start.4
  615.7 12.1 %fusion.9 = f32[128,512]{1,0:T(8,128)S(1)} fusion(f32[128,512]{1,0:T(8,128)S(1)} %fusion, f32[3,8192,512]{2,1,0:T(8,128)} %param.9, f32[2,128,8192]{2,1,0:T(8,128)S(1)} %copy-done.1), kind=kOutput, calls=%fused_computation.12 | convolution fusion | flops 6442516480 | bytes 21495808 | tf_op jit(solution)/shard_map/dot_general | solution.py:12
  627.8 0.8 pad_maximum_fusion
  628.6 0.0 reduce-scatter.2.cloned.1.call-update
  628.6 35.0 %reduce-scatter.2.cloned.1.call-done = f32[16,1024]{1,0:T(8,128)} async-done(((f32[128,1024]{1,0:T(8,128)}), f32[16,1024]{1,0:T(8,128)}) %reduce-scatter.2.cloned.1.call-update) | async-done | bytes 65552 | tf_op jit(solution)/shard_map/reduce_scatter | solution.py:29
  663.6 0.0 copy-done.3
  663.7 0.0 copy-done.4
  663.7 1.5 multiply_reduce_fusion
  665.1 11.6 %all-reduce = (f32[2,16]{1,0:T(2,128)S(1)}, f32[2,16]{1,0:T(2,128)S(1)}) all-reduce(f32[2,16]{1,0:T(2,128)S(1)} %get-tuple-element.3, f32[2,16]{1,0:T(2,128)S(1)} %get-tuple-element.2), channel_id=1, replica_groups=mesh['layer'=2,'feat'=4,'width'=4] {'width'}, use_global_device_ids=true, to_apply=%region_2.0 | all-reduce | flops 64 | bytes 512 | tf_op jit(solution)/shard_map/psum | solution.py:40
  676.8 0.6 add_divide_fusion
Async XLA Ops:
  7.2 656.5 %reduce-scatter.2.cloned.1.call-start = ((), (), s32[]{:S(2)}) async-start(), calls=%async_computation.1 | async-start | bytes 589824 | tf_op jit(solution)/shard_map/reduce_scatter | solution.py:29
  22.8 3.2 copy-start
  26.0 553.7 %copy-start.2 = (f32[2,8192]{1,0:T(2,128)S(1)}, f32[2,8192]{1,0:T(2,128)}, u32[]{:S(2)}) copy-start(f32[2,8192]{1,0:T(2,128)} %param.8) | copy-start | bytes 196612
  26.0 181.7 %collective-permute-start = (f32[2,128,8192]{2,1,0:T(8,128)S(1)}, f32[2,128,8192]{2,1,0:T(8,128)}, u32[]{:S(2)}, u32[]{:S(2)}) collective-permute-start(f32[2,128,8192]{2,1,0:T(8,128)S(1)} %fusion.14), channel_id=1, source_target_pairs={{0,1},{1,0},{2,3},{3,2},{4,5},{5,4},{6,7},{7,6},{8,9},{9,8},{10,11... | collective-permute-start | bytes 25165832 | tf_op jit(solution)/shard_map/ppermute | solution.py:26
  218.0 361.7 %collective-permute-start.1 = (f32[2,128,8192]{2,1,0:T(8,128)}, f32[2,128,8192]{2,1,0:T(8,128)}, u32[]{:S(2)}, u32[]{:S(2)}) collective-permute-start(f32[2,128,8192]{2,1,0:T(8,128)} %add.40), channel_id=1, source_target_pairs={{0,2},{1,3},{2,0},{3,1},{4,6},{5,7},{6,4},{7,5},{8,10},{9,11},{10,... | collective-permute-start | bytes 25165832 | tf_op jit(solution)/shard_map/ppermute | solution.py:26
  590.8 13.0 %copy-start.1 = (f32[2,128,8192]{2,1,0:T(8,128)S(1)}, f32[2,128,8192]{2,1,0:T(8,128)}, u32[]{:S(2)}) copy-start(f32[2,128,8192]{2,1,0:T(8,128)} %add_maximum_fusion) | copy-start | bytes 25165828
  615.6 48.0 %copy-start.3 = (f32[2,16,512]{2,1,0:T(8,128)S(1)}, f32[2,16,512]{2,1,0:T(8,128)}, u32[]{:S(2)}) copy-start(f32[2,16,512]{2,1,0:T(8,128)} %param.11) | copy-start | bytes 196612
  615.6 48.0 %copy-start.4 = (f32[2,512]{1,0:T(2,128)S(1)}, f32[2,512]{1,0:T(2,128)}, u32[]{:S(2)}) copy-start(f32[2,512]{1,0:T(2,128)} %param.10) | copy-start | bytes 12292
Sparse Core Ops, SparseCore 0:
  628.8 34.8 reduce-scatter.1
